TPU v7x, 32 devices: a whole 2x2x4 slice. The times are simulated.
32 devices in a mesh: groups: 2 (over y), tm: 4 (over z), head: 4 (over x, core).
Axes of the slice: x: 2, y: 2, z: 4, core: 2. Of those that a mesh axis runs over, the one named last changes fastest.
Arguments:
- queries: bfloat16 [8, 256, 3072], P(('groups', 'tm'), 'head'), parts along dimension 0, may hold values from -128 to 128
- keys: bfloat16 [8, 256, 3072], P(('groups', 'tm'), 'head'), parts along dimension 0, may hold values from -6 to 6
- values: bfloat16 [8, 256, 3072], P(('groups', 'tm'), 'head'), parts along dimension 0, may hold values from -6 to 6
- residual: bfloat16 [8, 256, 5120], P(('groups', 'tm'), None, 'head'), parts along dimension 0, may hold values from -3 to 3
- fresh_frame: bfloat16 [512, 5120], P('groups', 'head'), parts along dimension 0, may hold values from -6 to 6
- out_weight: bfloat16 [3072, 5120], P('tm', 'head'), may hold values from -0.875 to 0.875
- time_weight: bfloat16 [256, 5120], P(None, 'head'), may hold values from -0.375 to 0.375
- noise_steps: int32 [8], P(('groups', 'tm')), parts along dimension 0, may hold values from 0 to 49, as said below
- frame_mask: int32 [8, 4], P(('groups', 'tm')), parts along dimension 0, may hold values from 0 to 1, as said below
Outputs:
- rolled: bfloat16 [8, 256, 5120], P(('groups', 'tm'), None, 'head'), parts along dimension 0
There are 2 independent parts, one for each index of `groups`. A program takes and returns all parts, laid end to end along the dimension named above; an argument that names none is the same for every part. Nothing has to cross between parts.
Inputs may be any that keep to these rules, and one draw needn't show every extreme that they name: frame_mask[i, j] is 1 exactly for i - L_i < j <= i, with a whole number L_i from 1 to 4 for each frame i; the last frame has L_i = 4. `noise_steps`: never falling along the frames; the first frame has 0 and the last 49.
All inputs are finite; a program needn't handle non-finite values.
Results may differ from a plain program's by a relative error of at most 0.0065.
Values may be sent and summed in bfloat16 or wider, within the bound.
A program may use at most 64 MiB of HBM per device.

v0:
```python
import math
import jax
import jax.numpy as jnp
from jax import lax
from jax.sharding import PartitionSpec as P

HD = 128
FREQ = 256
STEPS = 50


def shifted(value, axis, steps):
    count = lax.axis_size(axis)
    leading, last = (max(0, -steps), min(count, count - steps))
    return lax.ppermute(value, axis, [(source, source + steps) for source in range(leading, last)])


def time_features(noise_steps):
    timestep = 1000.0 * (noise_steps.astype(jnp.float32) + 1.0) / STEPS
    half = FREQ // 2
    rates = jnp.exp(-math.log(10000.0) * jnp.arange(half).astype(jnp.float32) / half)
    angles = timestep[:, None] * rates[None, :]
    return jnp.concatenate([jnp.cos(angles), jnp.sin(angles)], axis=1)


def on_device(
    queries, keys, values, residual, fresh_frame, out_weight, time_weight, noise_steps, frame_mask
):
    query_local, key_local, value_local = (
        lax.all_to_all(queries, "head", split_axis=2, concat_axis=1, tiled=True),
        lax.all_to_all(keys, "head", split_axis=2, concat_axis=1, tiled=True),
        lax.all_to_all(values, "head", split_axis=2, concat_axis=1, tiled=True),
    )
    tokens = query_local.shape[1]
    heads_here = query_local.shape[2] // HD
    scale = 1.0 / math.sqrt(HD)
    query_heads = query_local[0].reshape(tokens, heads_here, HD)
    key_value = jnp.stack([key_local[0], value_local[0]], axis=0)
    frame = lax.axis_index("tm")
    frames_total = lax.axis_size("tm")
    window = min(8, frames_total)
    mask_row = frame_mask[0]
    columns = jnp.arange(mask_row.shape[0], dtype=jnp.int32)

    def allowed_at(offset):
        hits = jnp.sum(jnp.where(columns == frame - offset, mask_row, 0))
        return hits > 0

    def absorb(state, block, allowed):
        running_max, weight_sum, accumulated = state
        key_heads = block[0].reshape(tokens, heads_here, HD)
        value_heads = block[1].reshape(tokens, heads_here, HD)
        scores = (
            jnp.einsum("qhd,khd->hqk", query_heads, key_heads, preferred_element_type=jnp.float32)
            * scale
        )
        new_max = jnp.where(allowed, jnp.maximum(running_max, jnp.max(scores, axis=2)), running_max)
        lifted = jnp.where(allowed, jnp.exp(jnp.minimum(scores - new_max[:, :, None], 0.0)), 0.0)
        factor = jnp.exp(running_max - new_max)
        weight_sum = weight_sum * factor + jnp.sum(lifted, axis=2)
        rounded = lifted.astype(jnp.bfloat16)
        accumulated = accumulated * jnp.transpose(factor)[:, :, None] + jnp.einsum(
            "hqk,khd->qhd", rounded, value_heads, preferred_element_type=jnp.float32
        )
        return (new_max, weight_sum, accumulated)

    state = (
        jnp.full((heads_here, tokens), -1e30, jnp.float32),
        jnp.zeros((heads_here, tokens), jnp.float32),
        jnp.zeros((tokens, heads_here, HD), jnp.float32),
    )
    state = absorb(state, key_value, allowed_at(0))
    moving = key_value
    for offset in range(1, window):
        moving = shifted(moving, "tm", 1)
        state = absorb(state, moving, allowed_at(offset))
    running_max, weight_sum, accumulated = state
    attention = (
        (accumulated / jnp.transpose(weight_sum)[:, :, None])
        .reshape(tokens, heads_here * HD)
        .astype(jnp.bfloat16)
    )
    weight_cols = lax.all_gather(out_weight, "tm", axis=0, tiled=True)
    projected = jnp.dot(
        lax.all_gather(attention, "head", axis=1, tiled=True),
        weight_cols,
        preferred_element_type=jnp.float32,
    )
    gate = jnp.dot(
        time_features(noise_steps), time_weight.astype(jnp.float32), precision=lax.Precision.HIGHEST
    )
    updated = (residual[0].astype(jnp.float32) + gate * projected).astype(jnp.bfloat16)
    moved = shifted(updated, "tm", -1)
    rolled = jnp.where(frame == frames_total - 1, fresh_frame, moved)
    return rolled[None]


def solution(mesh):
    placed = (
        P(("groups", "tm"), "head", None),
        P(("groups", "tm"), "head", None),
        P(("groups", "tm"), "head", None),
        P(("groups", "tm"), None, "head"),
        P("groups", "head"),
        P("tm", "head"),
        P(None, "head"),
        P(("groups", "tm")),
        P(("groups", "tm"), None),
    )
    return jax.shard_map(
        on_device,
        mesh=mesh,
        in_specs=placed,
        out_specs=P(("groups", "tm"), None, "head"),
        check_vma=False,
    )
```

profile of v0, /device:TPU:0, one launch (start us, length us, event | category | flops | bytes accessed | tf_op | source)
XLA Modules:
  0.0 350.7 jit_solution(9926861367071621732)
XLA Ops:
  6.5 3.6 %copy.96 = bf16[1,64,3072]{1,0,2:T(2,128)(2,1)S(1)} copy(bf16[1,64,3072]{2,1,0:T(8,128)(2,1)} %param.10) | data formatting | bytes 786432 | tf_op args[1]
  10.7 16.9 %reduce.3 = bf16[3072,64]{1,0:T(8,128)(2,1)S(1)} reduce(bf16[3072,1,64]{2,1,0:T(2,128)(2,1)S(1)} %bitcast.180, bf16[]{:T(256)} %broadcast.158), dimensions={1}, to_apply=%bitcast.157.reduce_sub_computation | reduce | bytes 786434
  27.6 1.3 reshape.82
  28.9 4.2 %all-to-all-start.1 = ((bf16[4,2,24576]{2,1,0:T(2,128)(2,1)}), bf16[4,2,24576]{2,1,0:T(2,128)(2,1)S(1)}, u32[]{:S(2)}, u32[]{:S(2)}) async-start(bf16[4,2,24576]{2,1,0:T(2,128)(2,1)} %reshape.82), calls=%async_computation.1 | async-start | bytes 786432 | tf_op jit(solution)/shard_map/all_to_all | solution.py:31
  33.1 3.6 %copy.102 = bf16[1,64,3072]{1,0,2:T(2,128)(2,1)S(1)} copy(bf16[1,64,3072]{2,1,0:T(8,128)(2,1)} %param.11) | data formatting | bytes 786432 | tf_op args[2]
  36.7 16.9 %reduce.2 = bf16[3072,64]{1,0:T(8,128)(2,1)S(1)} reduce(bf16[3072,1,64]{2,1,0:T(2,128)(2,1)S(1)} %bitcast.182, bf16[]{:T(256)} %broadcast.158), dimensions={1}, to_apply=%bitcast.155.reduce_sub_computation | reduce | bytes 786434
  53.6 1.3 reshape.80
  54.9 3.6 %all-to-all-start.2 = ((bf16[4,2,24576]{2,1,0:T(2,128)(2,1)}), bf16[4,2,24576]{2,1,0:T(2,128)(2,1)S(1)}, u32[]{:S(2)}, u32[]{:S(2)}) async-start(bf16[4,2,24576]{2,1,0:T(2,128)(2,1)} %reshape.80), calls=%async_computation.2 | async-start | bytes 786432 | tf_op jit(solution)/shard_map/all_to_all | solution.py:32
  59.3 1.5 copy.97
  61.2 4.8 %all-to-all-done.2 = bf16[4,2,24576]{2,1,0:T(2,128)(2,1)S(1)} async-done(((bf16[4,2,24576]{2,1,0:T(2,128)(2,1)}), bf16[4,2,24576]{2,1,0:T(2,128)(2,1)S(1)}, u32[]{:S(2)}, u32[]{:S(2)}) %all-to-all-start.2) | async-done | bytes 393248 | tf_op jit(solution)/shard_map/all_to_all | solution.py:32
  66.7 1.5 copy.103
  69.5 5.1 %collective-permute-start = (bf16[2,256,768]{2,1,0:T(8,128)(2,1)}, bf16[2,256,768]{2,1,0:T(8,128)(2,1)}, u32[]{:S(2)}, u32[]{:S(2)}) collective-permute-start(bf16[2,256,768]{2,1,0:T(8,128)(2,1)} %pad_maximum_fusion), channel_id=1, source_target_pairs={{0,4},{4,8},{8,12},{1,5},{5,9},{9,13},{2,6},{6,10},{10,14},{3,7},{... | collective-permute-start | bytes 2359304 | tf_op jit(solution)/shard_map/ppermute | solution.py:15
  74.6 1.8 copy.93
  76.4 17.8 %reduce.4 = bf16[3072,64]{1,0:T(8,128)(2,1)} reduce(bf16[3072,1,64]{2,1,0:T(2,128)(2,1)S(1)} %bitcast.181, bf16[]{:T(256)} %broadcast.158), dimensions={1}, to_apply=%bitcast.159.reduce_sub_computation | reduce | bytes 786434
  94.2 2.4 reshape.84
  96.7 3.5 all-to-all-start
  100.2 3.7 %collective-permute-start.1 = (bf16[2,256,768]{2,1,0:T(8,128)(2,1)}, bf16[2,256,768]{2,1,0:T(8,128)(2,1)}, u32[]{:S(2)}, u32[]{:S(2)}) collective-permute-start(bf16[2,256,768]{2,1,0:T(8,128)(2,1)} %collective-permute-done), channel_id=1, source_target_pairs={{0,4},{4,8},{8,12},{1,5},{5,9},{9,13},{2,6},{6,10},{10,14},{3,7},{... | collective-permute-start | bytes 2359304 | tf_op jit(solution)/shard_map/ppermute | solution.py:15
  110.0 1.5 copy.94
  113.6 2.1 fusion.74
  118.0 2.8 collective-permute-done.1
  120.7 5.3 %collective-permute-start.2 = (bf16[2,256,768]{2,1,0:T(8,128)(2,1)}, bf16[2,256,768]{2,1,0:T(8,128)(2,1)}, u32[]{:S(2)}, u32[]{:S(2)}) collective-permute-start(bf16[2,256,768]{2,1,0:T(8,128)(2,1)} %collective-permute-done.1), channel_id=1, source_target_pairs={{0,4},{4,8},{8,12},{1,5},{5,9},{9,13},{2,6},{6,10},{10,14},{3,7},{... | collective-permute-start | bytes 2359304 | tf_op jit(solution)/shard_map/ppermute | solution.py:15
  126.4 1.9 fusion.72
  130.5 1.6 bitcast_reduce_fusion.1
  132.0 9.9 %collective-permute-done.2 = bf16[2,256,768]{2,1,0:T(8,128)(2,1)} collective-permute-done((bf16[2,256,768]{2,1,0:T(8,128)(2,1)}, bf16[2,256,768]{2,1,0:T(8,128)(2,1)}, u32[]{:S(2)}, u32[]{:S(2)}) %collective-permute-start.2) | collective-permute-done | bytes 786464 | tf_op jit(solution)/shard_map/ppermute | solution.py:15
  141.9 1.9 fusion.71
  145.0 2.2 bitcast_reduce_fusion
  148.1 2.2 fusion.20
  156.9 18.9 %all-gather.3.cloned.1.call-done = bf16[256,3072]{0,1:T(8,128)(2,1)} async-done(((bf16[256,768]{0,1:T(8,128)(2,1)}), bf16[256,3072]{0,1:T(8,128)(2,1)}) %all-gather.3.cloned.1.call-update) | async-done | bytes 1572880 | tf_op jit(solution)/shard_map/all_gather | solution.py:85
  175.8 142.6 %all-gather.5.cloned.1.call-done = bf16[3072,1280]{1,0:T(8,128)(2,1)} async-done(((bf16[768,1280]{1,0:T(8,128)(2,1)}), bf16[3072,1280]{1,0:T(8,128)(2,1)}) %all-gather.5.cloned.1.call-update) | async-done | bytes 7864336 | tf_op jit(solution)/shard_map/all_gather | solution.py:83
  318.5 6.0 %fusion.1 = bf16[256,1280]{1,0:T(8,128)(2,1)S(1)} fusion(bf16[256,3072]{0,1:T(8,128)(2,1)} %all-gather.3.cloned.1.call-done, bf16[3072,1280]{1,0:T(8,128)(2,1)} %all-gather.5.cloned.1.call-done, bf16[1,256,1280]{2,1,0:T(8,128)(2,1)S(1)} %copy-done.8, f32[1280]{0:T(1024)S(1)} %convolution_reduce_fusion), kind=kOutput, calls=%fused_computation.2 | convolution fusion | flops 2014576640 | bytes 10753024 | tf_op jit(solution)/shard_map/dot_general | solution.py:84
  324.4 1.3 collective-permute-start.3
  325.7 17.2 %collective-permute-done.3 = bf16[256,1280]{1,0:T(8,128)(2,1)S(1)} collective-permute-done((bf16[256,1280]{1,0:T(8,128)(2,1)S(1)}, bf16[256,1280]{1,0:T(8,128)(2,1)S(1)}, u32[]{:S(2)}, u32[]{:S(2)}) %collective-permute-start.3) | collective-permute-done | bytes 655392 | tf_op jit(solution)/shard_map/ppermute | solution.py:15
  (67 shorter events, 22.8 us)
Async XLA Ops:
  6.5 149.9 %copy-start = (bf16[256,1280]{1,0:T(8,128)(2,1)S(1)}, bf16[256,1280]{1,0:T(8,128)(2,1)}, u32[]{:S(2)}) copy-start(bf16[256,1280]{1,0:T(8,128)(2,1)} %param.15) | copy-start | bytes 1966084
  28.9 26.0 %all-to-all-start.1 = ((bf16[4,2,24576]{2,1,0:T(2,128)(2,1)}), bf16[4,2,24576]{2,1,0:T(2,128)(2,1)S(1)}, u32[]{:S(2)}, u32[]{:S(2)}) async-start(bf16[4,2,24576]{2,1,0:T(2,128)(2,1)} %reshape.82), calls=%async_computation.1 | async-start | bytes 786432 | tf_op jit(solution)/shard_map/all_to_all | solution.py:31
  54.9 11.1 %all-to-all-start.2 = ((bf16[4,2,24576]{2,1,0:T(2,128)(2,1)}), bf16[4,2,24576]{2,1,0:T(2,128)(2,1)S(1)}, u32[]{:S(2)}, u32[]{:S(2)}) async-start(bf16[4,2,24576]{2,1,0:T(2,128)(2,1)} %reshape.80), calls=%async_computation.2 | async-start | bytes 786432 | tf_op jit(solution)/shard_map/all_to_all | solution.py:32
  68.2 6.3 %copy-start.10 = (bf16[1,64,3072]{2,1,0:T(8,128)(2,1)S(1)}, bf16[1,64,3072]{2,1,0:T(8,128)(2,1)}, u32[]{:S(2)}) copy-start(bf16[1,64,3072]{2,1,0:T(8,128)(2,1)} %param.9) | copy-start | bytes 1179652
  69.5 30.7 %collective-permute-start = (bf16[2,256,768]{2,1,0:T(8,128)(2,1)}, bf16[2,256,768]{2,1,0:T(8,128)(2,1)}, u32[]{:S(2)}, u32[]{:S(2)}) collective-permute-start(bf16[2,256,768]{2,1,0:T(8,128)(2,1)} %pad_maximum_fusion), channel_id=1, source_target_pairs={{0,4},{4,8},{8,12},{1,5},{5,9},{9,13},{2,6},{6,10},{10,14},{3,7},{... | collective-permute-start | bytes 2359304 | tf_op jit(solution)/shard_map/ppermute | solution.py:15
  94.2 9.7 %copy-start.12 = (s32[1,4]{1,0:T(1,128)S(1)}, s32[1,4]{1,0:T(1,128)}, u32[]{:S(2)}) copy-start(s32[1,4]{1,0:T(1,128)} %param.17) | copy-start | bytes 52
  96.7 12.5 %all-to-all-start = ((bf16[4,2,24576]{2,1,0:T(2,128)(2,1)}), bf16[4,2,24576]{2,1,0:T(2,128)(2,1)S(1)}, u32[]{:S(2)}, u32[]{:S(2)}) async-start(bf16[4,2,24576]{2,1,0:T(2,128)(2,1)} %reshape.84), calls=%async_computation | async-start | bytes 786432 | tf_op jit(solution)/shard_map/all_to_all | solution.py:30
  100.1 75.7 %all-gather.3.cloned.1.call-start = ((), (), s32[]{:S(2)}) async-start(), calls=%async_computation.3 | async-start | bytes 1966080 | tf_op jit(solution)/shard_map/all_gather | solution.py:85
  100.2 20.5 %collective-permute-start.1 = (bf16[2,256,768]{2,1,0:T(8,128)(2,1)}, bf16[2,256,768]{2,1,0:T(8,128)(2,1)}, u32[]{:S(2)}, u32[]{:S(2)}) collective-permute-start(bf16[2,256,768]{2,1,0:T(8,128)(2,1)} %collective-permute-done), channel_id=1, source_target_pairs={{0,4},{4,8},{8,12},{1,5},{5,9},{9,13},{2,6},{6,10},{10,14},{3,7},{... | collective-permute-start | bytes 2359304 | tf_op jit(solution)/shard_map/ppermute | solution.py:15
  111.8 1.8 copy-start.4
  120.7 21.2 %collective-permute-start.2 = (bf16[2,256,768]{2,1,0:T(8,128)(2,1)}, bf16[2,256,768]{2,1,0:T(8,128)(2,1)}, u32[]{:S(2)}, u32[]{:S(2)}) collective-permute-start(bf16[2,256,768]{2,1,0:T(8,128)(2,1)} %collective-permute-done.1), channel_id=1, source_target_pairs={{0,4},{4,8},{8,12},{1,5},{5,9},{9,13},{2,6},{6,10},{10,14},{3,7},{... | collective-permute-start | bytes 2359304 | tf_op jit(solution)/shard_map/ppermute | solution.py:15
  148.1 2.2 copy-start.1
  148.1 2.3 copy-start.3
  150.4 0.7 copy-start.11
  150.4 1.4 copy-start.2
  150.4 1.5 copy-start.9
  151.1 1.3 copy-start.5
  152.4 1.0 copy-start.6
  155.0 163.5 %copy-start.8 = (bf16[1,256,1280]{2,1,0:T(8,128)(2,1)S(1)}, bf16[1,256,1280]{2,1,0:T(8,128)(2,1)}, u32[]{:S(2)}) copy-start(bf16[1,256,1280]{2,1,0:T(8,128)(2,1)} %param.12) | copy-start | bytes 1966084
  155.0 163.4 %all-gather.5.cloned.1.call-start = ((), (), s32[]{:S(2)}) async-start(), calls=%async_computation.4 | async-start | bytes 9830400 | tf_op jit(solution)/shard_map/all_gather | solution.py:83
  156.9 186.1 %copy-start.7 = (bf16[256,1280]{1,0:T(8,128)(2,1)S(1)}, bf16[256,1280]{1,0:T(8,128)(2,1)}, u32[]{:S(2)}) copy-start(bf16[256,1280]{1,0:T(8,128)(2,1)} %param.13) | copy-start | bytes 1966084
  324.4 18.5 %collective-permute-start.3 = (bf16[256,1280]{1,0:T(8,128)(2,1)S(1)}, bf16[256,1280]{1,0:T(8,128)(2,1)S(1)}, u32[]{:S(2)}, u32[]{:S(2)}) collective-permute-start(bf16[256,1280]{1,0:T(8,128)(2,1)S(1)} %fusion.1), channel_id=1, source_target_pairs={{4,0},{8,4},{12,8},{5,1},{9,5},{13,9},{6,2},{10,6},{14,10},{7,3},{... | collective-permute-start | bytes 1966088 | tf_op jit(solution)/shard_map/ppermute | solution.py:15
Sparse Core Ops, SparseCore 0:
  155.1 20.6 all-gather.2
  177.4 141.0 all-gather.4
where the time goes:
time: 352 us; the launch traced here: 351 us
  waiting for transfers between devices  197 us (56%)
  other arithmetic  57.8 us (16%)
  local copies, waits for them, and re-layouts  37.1 us (11%)
  starting transfers between devices  26.8 us (8%)
  between operations  17 us (5%)
  matrix products  15.1 us (4%)
    all_gather x1, waiting for transfers between devices, on_device(): weight_cols = lax.all_gather(out_weight, 'tm', axis=0, tiled=True)  143 us
    unnamed x3, other arithmetic  51.6 us
    ppermute x4, waiting for transfers between devices, shifted(): lax.ppermute(value, axis, [(source, source + steps) for source in range(l...  29.9 us
    all_gather x1, waiting for transfers between devices, on_device(): lax.all_gather(attention, 'head', axis=1, tiled=True)  18.9 us
    unnamed x36, local copies, waits for them, and re-layouts  18.5 us
    ppermute x4, starting transfers between devices, shifted(): lax.ppermute(value, axis, [(source, source + steps) for source in range(l...  15.3 us
  transfers between devices with their start and end apart: 9, of which 6 were waited for; matrix products, arithmetic and copies ran while one was open for 18% of the time, Pallas kernels for 0%

commit v1 on v0

--- a/solution.py
+++ b/solution.py
@@ -80,7 +80,12 @@
         .reshape(tokens, heads_here * HD)
         .astype(jnp.bfloat16)
     )
-    weight_cols = lax.all_gather(out_weight, "tm", axis=0, tiled=True)
+    ring = [out_weight]
+    for hop in range(3):
+        ring.append(lax.ppermute(ring[-1], "tm", [(dev, (dev + 1) % 4) for dev in range(4)]))
+    weight_cols = jnp.roll(
+        jnp.concatenate(ring[::-1], axis=0), (lax.axis_index("tm") + 1) * ring[0].shape[0], axis=0
+    )
     projected = jnp.dot(
         lax.all_gather(attention, "head", axis=1, tiled=True),
         weight_cols,

time: 352 us -> 291 us (0.83)
  waiting for transfers between devices: 197 us -> 114 us
  local copies, waits for them, and re-layouts: 37.1 us -> 58.1 us
  starting transfers between devices: 26.8 us -> 30.9 us
    all_gather x1 -> x0, waiting for transfers between devices: 143 us -> none  [on_device(): weight_cols = lax.all_gather(out_weight, 'tm', axis=0, tiled=True)]
    ppermute x4, waiting for transfers between devices: 29.9 us -> 71.3 us  [shifted(): lax.ppermute(value, axis, [(source, source + steps) for source in range(l...]
    ppermute x0 -> x3, waiting for transfers between devices: none -> 37.6 us  [on_device(): lax.ppermute(ring[-1], 'tm', [(dev, (dev + 1) % 4) for dev in range(4)])]
    unnamed x36 -> x47, local copies, waits for them, and re-layouts: 18.5 us -> 38.8 us
    all_gather x1, waiting for transfers between devices: 18.9 us -> 0.01 us  [on_device(): lax.all_gather(attention, 'head', axis=1, tiled=True)]
    ppermute x0 -> x3, starting transfers between devices: none -> 5.65 us  [on_device(): lax.ppermute(ring[-1], 'tm', [(dev, (dev + 1) % 4) for dev in range(4)])]
    all_to_all x1, waiting for transfers between devices: 4.77 us -> 0.01 us  [on_device(): lax.all_to_all(values, 'head', split_axis=2, concat_axis=1, tiled=True)]
    all_to_all x1, waiting for transfers between devices: 0.01 us -> 4.77 us  [on_device(): lax.all_to_all(keys, 'head', split_axis=2, concat_axis=1, tiled=True)]
  transfers between devices with their start and end apart: 9 -> 11, of which waited for: 6 -> 5; matrix products, arithmetic and copies ran while one was open for 18% -> 41% of each run, Pallas kernels for 0% -> 0%
where the time goes in v1:
time: 291 us; the launch traced here: 290 us
  waiting for transfers between devices  114 us (39%)
  local copies, waits for them, and re-layouts  58.1 us (20%)
  other arithmetic  55.5 us (19%)
  starting transfers between devices  30.9 us (11%)
  between operations  16.9 us (6%)
  matrix products  15.1 us (5%)
    ppermute x4, waiting for transfers between devices, shifted(): lax.ppermute(value, axis, [(source, source + steps) for source in range(l...  71.3 us
    unnamed x3, other arithmetic  51.6 us
    unnamed x47, local copies, waits for them, and re-layouts  38.8 us
    ppermute x3, waiting for transfers between devices, on_device(): lax.ppermute(ring[-1], 'tm', [(dev, (dev + 1) % 4) for dev in range(4)])  37.6 us
    ppermute x4, starting transfers between devices, shifted(): lax.ppermute(value, axis, [(source, source + steps) for source in range(l...  14.7 us
    slice x6, local copies, waits for them, and re-layouts, absorb(): value_heads = block[1].reshape(tokens, heads_here, HD)  8.13 us
    dot_general x1, matrix products, on_device(): jnp.dot(lax.all_gather(attention, 'head', axis=1, tiled=True), weight_col...  6.07 us
  transfers between devices with their start and end apart: 11, of which 5 were waited for; matrix products, arithmetic and copies ran while one was open for 41% of the time, Pallas kernels for 0%

profile of v1, /device:TPU:0, one launch (start us, length us, event | category | flops | bytes accessed | tf_op | source)
XLA Modules:
  0.0 290.2 jit_solution(8865766849988917208)
XLA Ops:
  6.5 3.1 %collective-permute-start.3 = (bf16[768,1280]{1,0:T(8,128)(2,1)}, bf16[768,1280]{1,0:T(8,128)(2,1)}, u32[]{:S(2)}, u32[]{:S(2)}) collective-permute-start(bf16[768,1280]{1,0:T(8,128)(2,1)} %param.14), channel_id=1, source_target_pairs={{0,4},{4,8},{8,12},{12,0},{1,5},{5,9},{9,13},{13,1},{2,6},{6,10},{... | collective-permute-start | bytes 5898248 | tf_op jit(solution)/shard_map/ppermute | solution.py:85
  9.6 3.6 %copy.102 = bf16[1,64,3072]{1,0,2:T(2,128)(2,1)S(1)} copy(bf16[1,64,3072]{2,1,0:T(8,128)(2,1)} %param.11) | data formatting | bytes 786432 | tf_op args[2]
  13.7 16.9 %reduce.2 = bf16[3072,64]{1,0:T(8,128)(2,1)S(1)} reduce(bf16[3072,1,64]{2,1,0:T(2,128)(2,1)S(1)} %bitcast.179, bf16[]{:T(256)} %broadcast.158), dimensions={1}, to_apply=%bitcast.155.reduce_sub_computation | reduce | bytes 786434
  31.9 3.6 %all-to-all-start.2 = ((bf16[4,2,24576]{2,1,0:T(2,128)(2,1)}), bf16[4,2,24576]{2,1,0:T(2,128)(2,1)S(1)}, u32[]{:S(2)}, u32[]{:S(2)}) async-start(bf16[4,2,24576]{2,1,0:T(2,128)(2,1)} %reshape.80), calls=%async_computation.2 | async-start | bytes 786432 | tf_op jit(solution)/shard_map/all_to_all | solution.py:32
  35.5 3.6 %copy.96 = bf16[1,64,3072]{1,0,2:T(2,128)(2,1)S(1)} copy(bf16[1,64,3072]{2,1,0:T(8,128)(2,1)} %param.10) | data formatting | bytes 786432 | tf_op args[1]
  39.1 16.9 %reduce.3 = bf16[3072,64]{1,0:T(8,128)(2,1)S(1)} reduce(bf16[3072,1,64]{2,1,0:T(2,128)(2,1)S(1)} %bitcast.181, bf16[]{:T(256)} %broadcast.158), dimensions={1}, to_apply=%bitcast.157.reduce_sub_computation | reduce | bytes 786434
  57.3 3.5 %all-to-all-start.1 = ((bf16[4,2,24576]{2,1,0:T(2,128)(2,1)}), bf16[4,2,24576]{2,1,0:T(2,128)(2,1)S(1)}, u32[]{:S(2)}, u32[]{:S(2)}) async-start(bf16[4,2,24576]{2,1,0:T(2,128)(2,1)} %reshape.82), calls=%async_computation.1 | async-start | bytes 786432 | tf_op jit(solution)/shard_map/all_to_all | solution.py:31
  61.6 1.5 copy.103
  63.4 4.8 %all-to-all-done.1 = bf16[4,2,24576]{2,1,0:T(2,128)(2,1)S(1)} async-done(((bf16[4,2,24576]{2,1,0:T(2,128)(2,1)}), bf16[4,2,24576]{2,1,0:T(2,128)(2,1)S(1)}, u32[]{:S(2)}, u32[]{:S(2)}) %all-to-all-start.1) | async-done | bytes 393248 | tf_op jit(solution)/shard_map/all_to_all | solution.py:31
  68.9 1.5 copy.97
  71.8 4.4 %collective-permute-start = (bf16[2,256,768]{2,1,0:T(8,128)(2,1)}, bf16[2,256,768]{2,1,0:T(8,128)(2,1)}, u32[]{:S(2)}, u32[]{:S(2)}) collective-permute-start(bf16[2,256,768]{2,1,0:T(8,128)(2,1)} %pad_maximum_fusion), channel_id=1, source_target_pairs={{0,4},{4,8},{8,12},{1,5},{5,9},{9,13},{2,6},{6,10},{10,14},{3,7},{... | collective-permute-start | bytes 2359304 | tf_op jit(solution)/shard_map/ppermute | solution.py:15
  76.2 1.8 copy.93
  78.0 17.8 %reduce.4 = bf16[3072,64]{1,0:T(8,128)(2,1)} reduce(bf16[3072,1,64]{2,1,0:T(2,128)(2,1)S(1)} %bitcast.180, bf16[]{:T(256)} %broadcast.158), dimensions={1}, to_apply=%bitcast.159.reduce_sub_computation | reduce | bytes 786434
  95.8 2.4 reshape.84
  98.2 3.5 %all-to-all-start = ((bf16[4,2,24576]{2,1,0:T(2,128)(2,1)}), bf16[4,2,24576]{2,1,0:T(2,128)(2,1)S(1)}, u32[]{:S(2)}, u32[]{:S(2)}) async-start(bf16[4,2,24576]{2,1,0:T(2,128)(2,1)} %reshape.84), calls=%async_computation | async-start | bytes 786432 | tf_op jit(solution)/shard_map/all_to_all | solution.py:30
  105.6 3.8 %collective-permute-start.1 = (bf16[2,256,768]{2,1,0:T(8,128)(2,1)}, bf16[2,256,768]{2,1,0:T(8,128)(2,1)}, u32[]{:S(2)}, u32[]{:S(2)}) collective-permute-start(bf16[2,256,768]{2,1,0:T(8,128)(2,1)} %collective-permute-done), channel_id=1, source_target_pairs={{0,4},{4,8},{8,12},{1,5},{5,9},{9,13},{2,6},{6,10},{10,14},{3,7},{... | collective-permute-start | bytes 2359304 | tf_op jit(solution)/shard_map/ppermute | solution.py:15
  114.1 2.1 fusion.84
  120.4 6.4 %collective-permute-done.1 = bf16[2,256,768]{2,1,0:T(8,128)(2,1)} collective-permute-done((bf16[2,256,768]{2,1,0:T(8,128)(2,1)}, bf16[2,256,768]{2,1,0:T(8,128)(2,1)}, u32[]{:S(2)}, u32[]{:S(2)}) %collective-permute-start.1) | collective-permute-done | bytes 786464 | tf_op jit(solution)/shard_map/ppermute | solution.py:15
  126.7 5.3 %collective-permute-start.2 = (bf16[2,256,768]{2,1,0:T(8,128)(2,1)}, bf16[2,256,768]{2,1,0:T(8,128)(2,1)}, u32[]{:S(2)}, u32[]{:S(2)}) collective-permute-start(bf16[2,256,768]{2,1,0:T(8,128)(2,1)} %collective-permute-done.1), channel_id=1, source_target_pairs={{0,4},{4,8},{8,12},{1,5},{5,9},{9,13},{2,6},{6,10},{10,14},{3,7},{... | collective-permute-start | bytes 2359304 | tf_op jit(solution)/shard_map/ppermute | solution.py:15
  136.2 49.0 %collective-permute-done.2 = bf16[2,256,768]{2,1,0:T(8,128)(2,1)} collective-permute-done((bf16[2,256,768]{2,1,0:T(8,128)(2,1)}, bf16[2,256,768]{2,1,0:T(8,128)(2,1)}, u32[]{:S(2)}, u32[]{:S(2)}) %collective-permute-start.2) | collective-permute-done | bytes 786464 | tf_op jit(solution)/shard_map/ppermute | solution.py:15
  185.1 2.1 fusion.81
  188.4 1.9 copy.122
  191.8 2.5 collective-permute-start.5
  200.6 37.6 %collective-permute-done.5 = bf16[768,1280]{1,0:T(8,128)(2,1)} collective-permute-done((bf16[768,1280]{1,0:T(8,128)(2,1)}, bf16[768,1280]{1,0:T(8,128)(2,1)}, u32[]{:S(2)}, u32[]{:S(2)}) %collective-permute-start.5) | collective-permute-done | bytes 1966112 | tf_op jit(solution)/shard_map/ppermute | solution.py:85
  238.3 3.0 %constant_dynamic-update-slice_fusion.7 = bf16[6144,1280]{1,0:T(8,128)(2,1)} fusion(bf16[768,1280]{1,0:T(8,128)(2,1)} %collective-permute-done.5), kind=kLoop, calls=%fused_computation.73 | loop fusion | bytes 3932160
  241.2 3.0 %constant_dynamic-update-slice_fusion.6 = bf16[6144,1280]{1,0:T(8,128)(2,1)} fusion(bf16[6144,1280]{1,0:T(8,128)(2,1)} %constant_dynamic-update-slice_fusion.7, bf16[768,1280]{1,0:T(8,128)(2,1)} %collective-permute-done.4), kind=kLoop, calls=%fused_computation.72 | loop fusion | bytes 3932160
  244.2 3.1 %constant_dynamic-update-slice_fusion.5 = bf16[6144,1280]{1,0:T(8,128)(2,1)} fusion(bf16[6144,1280]{1,0:T(8,128)(2,1)} %constant_dynamic-update-slice_fusion.6, bf16[768,1280]{1,0:T(8,128)(2,1)} %collective-permute-done.3), kind=kLoop, calls=%fused_computation.71 | loop fusion | bytes 3932160
  248.7 3.0 %constant_dynamic-update-slice_fusion.3 = bf16[6144,1280]{1,0:T(8,128)(2,1)} fusion(bf16[6144,1280]{1,0:T(8,128)(2,1)} %constant_dynamic-update-slice_fusion.4, bf16[768,1280]{1,0:T(8,128)(2,1)} %collective-permute-done.5), kind=kLoop, calls=%fused_computation.69 | loop fusion | bytes 3932160
  251.7 2.9 %constant_dynamic-update-slice_fusion.2 = bf16[6144,1280]{1,0:T(8,128)(2,1)} fusion(bf16[6144,1280]{1,0:T(8,128)(2,1)} %constant_dynamic-update-slice_fusion.3, bf16[768,1280]{1,0:T(8,128)(2,1)} %collective-permute-done.4), kind=kLoop, calls=%fused_computation.68 | loop fusion | bytes 3932160
  254.6 3.1 %constant_dynamic-update-slice_fusion.1 = bf16[6144,1280]{1,0:T(8,128)(2,1)} fusion(bf16[6144,1280]{1,0:T(8,128)(2,1)} %constant_dynamic-update-slice_fusion.2, bf16[768,1280]{1,0:T(8,128)(2,1)} %collective-permute-done.3), kind=kLoop, calls=%fused_computation.67 | loop fusion | bytes 3932160
  259.1 6.1 %fusion.8 = bf16[256,1280]{1,0:T(8,128)(2,1)S(1)} fusion(bf16[256,3072]{0,1:T(8,128)(2,1)} %all-gather.2.cloned.1.call-done, bf16[6144,1280]{1,0:T(8,128)(2,1)} %constant_dynamic-update-slice_fusion, s32[]{:T(128)S(6)} %select_n.178, bf16[1,256,1280]{2,1,0:T(8,128)(2,1)S(1)} %copy-done.14, f32[1280]{0:T(1024)S(1)} %copy-done.12), kind=kOutput, calls=%fused_computation.4 | convolution fusion | flops 2014576640 | bytes 10753028 | tf_op jit(solution)/shard_map/dot_general | solution.py:89
  266.5 15.9 %collective-permute-done.6 = bf16[256,1280]{1,0:T(8,128)(2,1)S(1)} collective-permute-done((bf16[256,1280]{1,0:T(8,128)(2,1)S(1)}, bf16[256,1280]{1,0:T(8,128)(2,1)S(1)}, u32[]{:S(2)}, u32[]{:S(2)}) %collective-permute-start.6) | collective-permute-done | bytes 655392 | tf_op jit(solution)/shard_map/ppermute | solution.py:15
  (82 shorter events, 33.9 us)
Async XLA Ops:
  6.5 102.9 %copy-start = (bf16[256,1280]{1,0:T(8,128)(2,1)S(1)}, bf16[256,1280]{1,0:T(8,128)(2,1)}, u32[]{:S(2)}) copy-start(bf16[256,1280]{1,0:T(8,128)(2,1)} %param.15) | copy-start | bytes 1966084
  6.5 107.5 %collective-permute-start.3 = (bf16[768,1280]{1,0:T(8,128)(2,1)}, bf16[768,1280]{1,0:T(8,128)(2,1)}, u32[]{:S(2)}, u32[]{:S(2)}) collective-permute-start(bf16[768,1280]{1,0:T(8,128)(2,1)} %param.14), channel_id=1, source_target_pairs={{0,4},{4,8},{8,12},{12,0},{1,5},{5,9},{9,13},{13,1},{2,6},{6,10},{... | collective-permute-start | bytes 5898248 | tf_op jit(solution)/shard_map/ppermute | solution.py:85
  31.9 25.4 %all-to-all-start.2 = ((bf16[4,2,24576]{2,1,0:T(2,128)(2,1)}), bf16[4,2,24576]{2,1,0:T(2,128)(2,1)S(1)}, u32[]{:S(2)}, u32[]{:S(2)}) async-start(bf16[4,2,24576]{2,1,0:T(2,128)(2,1)} %reshape.80), calls=%async_computation.2 | async-start | bytes 786432 | tf_op jit(solution)/shard_map/all_to_all | solution.py:32
  57.3 10.8 %all-to-all-start.1 = ((bf16[4,2,24576]{2,1,0:T(2,128)(2,1)}), bf16[4,2,24576]{2,1,0:T(2,128)(2,1)S(1)}, u32[]{:S(2)}, u32[]{:S(2)}) async-start(bf16[4,2,24576]{2,1,0:T(2,128)(2,1)} %reshape.82), calls=%async_computation.1 | async-start | bytes 786432 | tf_op jit(solution)/shard_map/all_to_all | solution.py:31
  70.7 5.4 %copy-start.10 = (bf16[1,64,3072]{2,1,0:T(8,128)(2,1)S(1)}, bf16[1,64,3072]{2,1,0:T(8,128)(2,1)}, u32[]{:S(2)}) copy-start(bf16[1,64,3072]{2,1,0:T(8,128)(2,1)} %param.9) | copy-start | bytes 1179652
  71.8 33.8 %collective-permute-start = (bf16[2,256,768]{2,1,0:T(8,128)(2,1)}, bf16[2,256,768]{2,1,0:T(8,128)(2,1)}, u32[]{:S(2)}, u32[]{:S(2)}) collective-permute-start(bf16[2,256,768]{2,1,0:T(8,128)(2,1)} %pad_maximum_fusion), channel_id=1, source_target_pairs={{0,4},{4,8},{8,12},{1,5},{5,9},{9,13},{2,6},{6,10},{10,14},{3,7},{... | collective-permute-start | bytes 2359304 | tf_op jit(solution)/shard_map/ppermute | solution.py:15
  95.8 6.0 %copy-start.13 = (s32[1,4]{1,0:T(1,128)S(1)}, s32[1,4]{1,0:T(1,128)}, u32[]{:S(2)}) copy-start(s32[1,4]{1,0:T(1,128)} %param.17) | copy-start | bytes 52
  98.2 12.6 %all-to-all-start = ((bf16[4,2,24576]{2,1,0:T(2,128)(2,1)}), bf16[4,2,24576]{2,1,0:T(2,128)(2,1)S(1)}, u32[]{:S(2)}, u32[]{:S(2)}) async-start(bf16[4,2,24576]{2,1,0:T(2,128)(2,1)} %reshape.84), calls=%async_computation | async-start | bytes 786432 | tf_op jit(solution)/shard_map/all_to_all | solution.py:30
  101.7 157.4 %all-gather.2.cloned.1.call-start = ((), (), s32[]{:S(2)}) async-start(), calls=%async_computation.3 | async-start | bytes 1966080 | tf_op jit(solution)/shard_map/all_gather | solution.py:90
  105.6 21.1 %collective-permute-start.1 = (bf16[2,256,768]{2,1,0:T(8,128)(2,1)}, bf16[2,256,768]{2,1,0:T(8,128)(2,1)}, u32[]{:S(2)}, u32[]{:S(2)}) collective-permute-start(bf16[2,256,768]{2,1,0:T(8,128)(2,1)} %collective-permute-done), channel_id=1, source_target_pairs={{0,4},{4,8},{8,12},{1,5},{5,9},{9,13},{2,6},{6,10},{10,14},{3,7},{... | collective-permute-start | bytes 2359304 | tf_op jit(solution)/shard_map/ppermute | solution.py:15
  114.0 18.4 %copy-start.2 = (bf16[256,6,128]{2,1,0:T(8,128)(2,1)}, bf16[256,6,128]{2,1,0:T(8,128)(2,1)S(1)}, u32[]{:S(2)}) copy-start(bf16[256,6,128]{2,1,0:T(8,128)(2,1)S(1)} %reshape_squeeze.21) | copy-start | bytes 1179652
  114.0 77.8 %collective-permute-start.4 = (bf16[768,1280]{1,0:T(8,128)(2,1)}, bf16[768,1280]{1,0:T(8,128)(2,1)}, u32[]{:S(2)}, u32[]{:S(2)}) collective-permute-start(bf16[768,1280]{1,0:T(8,128)(2,1)} %collective-permute-done.3), channel_id=1, source_target_pairs={{0,4},{4,8},{8,12},{12,0},{1,5},{5,9},{9,13},{13,1},{2,6},{6,10},{... | collective-permute-start | bytes 5898248 | tf_op jit(solution)/shard_map/ppermute | solution.py:85
  126.7 58.4 %collective-permute-start.2 = (bf16[2,256,768]{2,1,0:T(8,128)(2,1)}, bf16[2,256,768]{2,1,0:T(8,128)(2,1)}, u32[]{:S(2)}, u32[]{:S(2)}) collective-permute-start(bf16[2,256,768]{2,1,0:T(8,128)(2,1)} %collective-permute-done.1), channel_id=1, source_target_pairs={{0,4},{4,8},{8,12},{1,5},{5,9},{9,13},{2,6},{6,10},{10,14},{3,7},{... | collective-permute-start | bytes 2359304 | tf_op jit(solution)/shard_map/ppermute | solution.py:15
  190.3 1.5 copy-start.11
  191.8 46.4 %collective-permute-start.5 = (bf16[768,1280]{1,0:T(8,128)(2,1)}, bf16[768,1280]{1,0:T(8,128)(2,1)}, u32[]{:S(2)}, u32[]{:S(2)}) collective-permute-start(bf16[768,1280]{1,0:T(8,128)(2,1)} %collective-permute-done.4), channel_id=1, source_target_pairs={{0,4},{4,8},{8,12},{12,0},{1,5},{5,9},{9,13},{13,1},{2,6},{6,10},{... | collective-permute-start | bytes 5898248 | tf_op jit(solution)/shard_map/ppermute | solution.py:85
  194.3 1.4 copy-start.4
  195.8 1.0 copy-start.9
  196.4 1.0 copy-start.5
  197.4 1.0 copy-start.6
  198.4 1.0 copy-start.8
  244.2 3.1 %copy-start.3 = (bf16[768,1280]{1,0:T(8,128)(2,1)S(1)}, bf16[768,1280]{1,0:T(8,128)(2,1)}, u32[]{:S(2)}) copy-start(bf16[768,1280]{1,0:T(8,128)(2,1)} %param.14) | copy-start | bytes 5898244
  257.7 1.4 copy-start.12
  257.7 1.4 copy-start.14
  259.1 23.3 %copy-start.7 = (bf16[256,1280]{1,0:T(8,128)(2,1)S(1)}, bf16[256,1280]{1,0:T(8,128)(2,1)}, u32[]{:S(2)}) copy-start(bf16[256,1280]{1,0:T(8,128)(2,1)} %param.13) | copy-start | bytes 1966084
  259.1 24.2 %copy-start.1 = (bf16[256,1280]{1,0:T(8,128)(2,1)S(1)}, bf16[256,1280]{1,0:T(8,128)(2,1)}, u32[]{:S(2)}) copy-start(bf16[256,1280]{1,0:T(8,128)(2,1)} %param.15) | copy-start | bytes 1966084
  265.2 17.2 %collective-permute-start.6 = (bf16[256,1280]{1,0:T(8,128)(2,1)S(1)}, bf16[256,1280]{1,0:T(8,128)(2,1)S(1)}, u32[]{:S(2)}, u32[]{:S(2)}) collective-permute-start(bf16[256,1280]{1,0:T(8,128)(2,1)S(1)} %fusion.8), channel_id=1, source_target_pairs={{4,0},{8,4},{12,8},{5,1},{9,5},{13,9},{6,2},{10,6},{14,10},{7,3},{... | collective-permute-start | bytes 1966088 | tf_op jit(solution)/shard_map/ppermute | solution.py:15
Sparse Core Ops, SparseCore 0:
  200.7 18.7 all-gather.1
